TPU v7x, 256 devices: a whole 4x4x8 slice. The times are simulated.
256 devices in a mesh: cell: 64 (over y, z, core), view: 4 (over x).
Axes of the slice: x: 4, y: 4, z: 8, core: 2. Of those that a mesh axis runs over, the one named last changes fastest.
Arguments:
- gaussians: float32 [1024, 9, 256], P('cell'), as said below
- seg_count: int32 [4, 64], P('view', 'cell'), may hold values from 1 to 3, as said below
- seg_block: int32 [4, 64, 3], P('view', 'cell'), may hold values from 0 to 1023, as said below
- ray_count: int32 [4, 64], P('view', 'cell'), may hold values from 576 to 2304
- camera_shift: float32 [4, 2], P('view'), may hold values from -6 to 6
- target: float32 [4, 64, 3, 2304], P('view', 'cell'), may hold values from 0 to 1
Outputs:
- image: float32 [4, 64, 3, 2304], P('view', 'cell')
- gauss_grad: float32 [1024, 9, 256], P('cell')
Inputs may be any that keep to these rules, and one draw needn't show every extreme that they name: `gaussians`: each column of a block is one Gaussian: a mean, the entries a, b, c of a positive definite inverse covariance, an opacity in (0, 1), three colours. `seg_count`: tiles 2m and 2m + 1 of a view hold 4 segments together; in every view some tile holds 3. Segment k of tile t uses a block stored in cell seg_block // 16, which is t + e modulo 64 for some e from -2 to 2; entries at k >= seg_count are not used.
All inputs are finite; a program needn't handle non-finite values.
Results may differ from a plain program's by a relative error of at most 0.0003.
Values sent between devices are 32-bit elements; how exact they have to be, the bound alone decides.
No kernel may reach another device: no remote copies, remote signals or barrier semaphores. Data moves between devices by JAX's collectives and lax.ppermute only.
A program may use at most 64 MiB of HBM per device.

v0:
```python
import jax
import jax.numpy as jnp
from jax import lax
from jax.sharding import PartitionSpec as P

TILE = 48
REACH = 2
precise = lax.Precision.HIGHEST


def shifted(block, axis, distance):
    devices = range(lax.axis_size(axis))
    route = [((i - distance) % len(devices), i) for i in devices]
    return lax.ppermute(block, axis, route)


def pixel_frame(shift, pixels):
    pixel_ids = jnp.arange(pixels)
    centre = (TILE - 1) / 2.0
    pix_x = (pixel_ids % TILE).astype(jnp.float32) - centre - shift[0]
    pix_y = (pixel_ids // TILE).astype(jnp.float32) - centre - shift[1]
    return (pix_x, pix_y)


def triangles(length):
    row_ids = lax.broadcasted_iota(jnp.int32, (length, length), 0)
    col_ids = lax.broadcasted_iota(jnp.int32, (length, length), 1)
    return ((col_ids < row_ids).astype(jnp.float32), (col_ids > row_ids).astype(jnp.float32))


def splat(params, pix_x, pix_y):
    delta_x = pix_x[None, :] - params[0][:, None]
    delta_y = pix_y[None, :] - params[1][:, None]
    quad_form = (
        params[2][:, None] * delta_x * delta_x
        + 2.0 * params[3][:, None] * delta_x * delta_y
        + params[4][:, None] * delta_y * delta_y
    )
    alphas = params[5][:, None] * jnp.exp(-0.5 * quad_form)
    return (alphas, jnp.log1p(-alphas))


def forward_task(params, pix_x, pix_y, lower_tri):
    alphas, log_trans = splat(params, pix_x, pix_y)
    prefix = jnp.dot(lower_tri, log_trans, precision=precise, preferred_element_type=jnp.float32)
    weights = alphas * jnp.exp(prefix)
    colour = jnp.dot(params[6:9], weights, precision=precise, preferred_element_type=jnp.float32)
    totals = jnp.sum(log_trans, axis=0)
    return jnp.concatenate([colour, totals[None, :]], axis=0)


def gradient_rows(params, pix_x, pix_y, weighted, weights, weight_cot):
    features = jnp.stack(
        [jnp.ones_like(pix_x), pix_x, pix_y, pix_x * pix_x, pix_x * pix_y, pix_y * pix_y]
    )
    moments = lax.dot_general(
        features,
        weighted,
        (((1,), (1,)), ((), ())),
        precision=precise,
        preferred_element_type=jnp.float32,
    )
    colour_grad = lax.dot_general(
        weight_cot,
        weights,
        (((1,), (1,)), ((), ())),
        precision=precise,
        preferred_element_type=jnp.float32,
    )
    mean_x, mean_y, conic_a, conic_b, conic_c, opacity = (
        params[0],
        params[1],
        params[2],
        params[3],
        params[4],
        params[5],
    )
    moment_zero = moments[0]
    along_x = moments[1] - mean_x * moment_zero
    along_y = moments[2] - mean_y * moment_zero
    square_x = moments[3] - 2.0 * mean_x * moments[1] + mean_x * mean_x * moment_zero
    cross_xy = (
        moments[4] - mean_x * moments[2] - mean_y * moments[1] + mean_x * mean_y * moment_zero
    )
    square_y = moments[5] - 2.0 * mean_y * moments[2] + mean_y * mean_y * moment_zero
    grad_rows = jnp.stack(
        [
            conic_a * along_x + conic_b * along_y,
            conic_b * along_x + conic_c * along_y,
            -0.5 * square_x,
            -cross_xy,
            -0.5 * square_y,
            moment_zero / opacity,
        ]
    )
    return jnp.concatenate([grad_rows, colour_grad], axis=0)


def backward_task(params, cotangent, pix_x, pix_y, lower_tri, upper_tri):
    alphas, log_trans = splat(params, pix_x, pix_y)
    transmit = jnp.exp(
        jnp.dot(lower_tri, log_trans, precision=precise, preferred_element_type=jnp.float32)
    )
    weights = alphas * transmit
    weight_cot = cotangent[:3]
    shaded = lax.dot_general(
        params[6:9],
        weight_cot,
        (((0,), (0,)), ((), ())),
        precision=precise,
        preferred_element_type=jnp.float32,
    )
    later_sum = jnp.dot(
        upper_tri, weights * shaded, precision=precise, preferred_element_type=jnp.float32
    )
    dalpha = transmit * shaded - (later_sum + cotangent[3][None, :]) / (1.0 - alphas)
    return gradient_rows(params, pix_x, pix_y, dalpha * alphas, weights, weight_cot)


def composite(partials, live_mask, target_tile, valid_slot):
    slot_total = partials.shape[0]
    running = jnp.zeros(partials.shape[2:], jnp.float32)
    transmit = []
    for slot_index in range(slot_total):
        transmit.append(jnp.exp(running))
        running = running + partials[slot_index, 3]
    transmit = jnp.stack(transmit)
    shaded = transmit[:, None, :] * partials[:, :3]
    rendered = jnp.sum(shaded, axis=0) * live_mask
    residual = (rendered - target_tile) * live_mask
    behind = []
    running_sum = jnp.zeros_like(rendered)
    for slot_index in range(slot_total - 1, -1, -1):
        behind.insert(0, running_sum)
        running_sum = running_sum + shaded[slot_index]
    behind = jnp.stack(behind)
    valid_weight = valid_slot.astype(jnp.float32)
    weight_cot = transmit[:, None, :] * residual[None] * valid_weight[:, None, None]
    after_cot = jnp.sum(residual[None] * behind, axis=1) * valid_weight[:, None]
    return (rendered, jnp.concatenate([weight_cot, after_cot[:, None, :]], axis=1))


def shards(gaussians, seg_count, seg_block, ray_count, camera_shift, target):
    cell_count = lax.axis_size("cell")
    cell_index = lax.axis_index("cell")
    per_block = gaussians.shape[0]
    pixels = target.shape[3]
    lower_tri, upper_tri = triangles(gaussians.shape[2])
    blocks = seg_block[0, 0]
    slot_count = blocks.shape[0]
    own_count = seg_count[0, 0]
    home_cell = blocks // per_block
    local_block = blocks % per_block
    offset = (home_cell - cell_index + REACH) % cell_count - REACH
    pix_x, pix_y = pixel_frame(camera_shift[0], pixels)
    valid_slot = jnp.arange(slot_count) < own_count

    def run_forward(params):
        return forward_task(params, pix_x, pix_y, lower_tri)

    def run_backward(bundle):
        return backward_task(bundle[0], bundle[1], pix_x, pix_y, lower_tri, upper_tri)

    near_list = []
    for shift_by in range(-REACH, REACH + 1):
        if shift_by == 0:
            near_list.append(gaussians)
        else:
            near_list.append(shifted(gaussians, "cell", -shift_by))
    near_stack = jnp.concatenate(near_list, axis=0)
    pick_index = (offset + REACH) * per_block + local_block
    own_params = jnp.take(near_stack, pick_index, axis=0)
    partials = lax.map(run_forward, own_params)
    partials = jnp.where(valid_slot[:, None, None], partials, 0.0)
    live_mask = (jnp.arange(pixels) < ray_count[0, 0]).astype(jnp.float32)
    rendered, cotangent = composite(partials, live_mask, target[0, 0], valid_slot)
    own_grads = lax.map(run_backward, (own_params, cotangent))
    spot_count = (2 * REACH + 1) * per_block
    onehot = (pick_index[:, None] == jnp.arange(spot_count)[None, :]).astype(jnp.float32)
    spread = jnp.einsum("sk,sjg->kjg", onehot, own_grads, precision=precise)
    spread = spread.reshape((2 * REACH + 1, per_block) + gaussians.shape[1:])
    block_grads = spread[REACH]
    for shift_by in range(-REACH, REACH + 1):
        if shift_by != 0:
            block_grads = block_grads + shifted(spread[shift_by + REACH], "cell", shift_by)
    gauss_grad = lax.psum(block_grads, "view")
    return (rendered[None, None], gauss_grad)


def solution(mesh):
    placed = (
        P("cell", None, None),
        P("view", "cell"),
        P("view", "cell", None),
        P("view", "cell"),
        P("view", None),
        P("view", "cell", None, None),
    )
    return jax.shard_map(
        shards,
        mesh=mesh,
        in_specs=placed,
        out_specs=(P("view", "cell", None, None), P("cell", None, None)),
        check_vma=False,
    )
```

profile of v0, /device:TPU:8, one launch (start us, length us, event | category | flops | bytes accessed | tf_op | source)
XLA Modules:
  0.0 183.9 jit_solution(16609155894614825310)
XLA Ops:
  10.2 3.9 %collective-permute-start.2 = (f32[16,9,256]{2,1,0:T(8,128)S(1)}, f32[16,9,256]{2,1,0:T(8,128)S(1)}, u32[]{:S(2)}, u32[]{:S(2)}) collective-permute-start(f32[16,9,256]{2,1,0:T(8,128)S(1)} %copy.22), channel_id=1, source_target_pairs={{4,0},{8,4},{12,8},{16,12},{20,16},{24,20},{28,24},{32,28},{36,32}... | collective-permute-start | bytes 442376 | tf_op jit(solution)/shard_map/ppermute | solution.py:14
  29.0 30.8 %while.26 = (s32[]{:T(128)}, f32[3,4,2304]{2,1,0:T(4,128)S(1)}, f32[3,9,256]{2,1,0:T(8,128)S(1)}, f32[]{:T(128)}, f32[]{:T(128)}) while((s32[]{:T(128)}, f32[3,4,2304]{2,1,0:T(4,128)S(1)}, f32[3,9,256]{2,1,0:T(8,128)S(1)}, f32[]{:T(128)}, f32[]{:T(128)}) %tuple.102), condition=%wide.region_2.3_spmd.clone.clone, body=%wide.region_0.2_spmd.clone.sunk.clone | while | flops 1856945664 | bytes 4940977 | solution.py:173
  30.2 4.6 %fusion.187 = f32[256,2304]{0,1:T(8,128)S(1)} fusion(f32[256]{0:T(256)S(1)} %bitcast.284, f32[256]{0:T(256)S(1)} %bitcast.276, f32[2304]{0:T(1024)S(1)} %get-tuple-element.382, f32[256]{0:T(256)S(1)} %bitcast.278, f32[256]{0:T(256)S(1)} %bitcast.280, f32[2304]{0:T(1024)S(1)} %get-tuple-element.385, f32[256]{0:T(256)S(1)} %bitcast.282, ...), kind=kOutput, calls=%fused_computation.19.clone.1.clone | convolution fusion | flops 1827405824 | bytes 2383872 | tf_op jit(solution)/shard_map/while/body/eval_jaxpr/dot_general | solution.py:45
  36.9 2.3 %fusion.186 = f32[2304]{0:T(1024)S(1)} fusion(f32[256]{0:T(256)S(1)} %bitcast.285, f32[256]{0:T(256)S(1)} %bitcast.277, f32[2304]{0:T(1024)S(1)} %get-tuple-element.382, f32[256]{0:T(256)S(1)} %bitcast.279, f32[256]{0:T(256)S(1)} %bitcast.281, f32[2304]{0:T(1024)S(1)} %get-tuple-element.385, f32[256]{0:T(256)S(1)} %bitcast.283, f32[256]{0:T(256)S(1)} %bitcast.275), kind=kLoop, calls=%fused_computation.26.clone.1.clone | loop fusion | flops 8255232 | bytes 33792 | tf_op jit(solution)/shard_map/while/body/eval_jaxpr/reduce_sum | solution.py:48
  40.5 4.6 %fusion.187 = f32[256,2304]{0,1:T(8,128)S(1)} fusion(f32[256]{0:T(256)S(1)} %bitcast.284, f32[256]{0:T(256)S(1)} %bitcast.276, f32[2304]{0:T(1024)S(1)} %get-tuple-element.382, f32[256]{0:T(256)S(1)} %bitcast.278, f32[256]{0:T(256)S(1)} %bitcast.280, f32[2304]{0:T(1024)S(1)} %get-tuple-element.385, f32[256]{0:T(256)S(1)} %bitcast.282, ...), kind=kOutput, calls=%fused_computation.19.clone.1.clone | convolution fusion | flops 1827405824 | bytes 2383872 | tf_op jit(solution)/shard_map/while/body/eval_jaxpr/dot_general | solution.py:45
  47.1 2.3 %fusion.186 = f32[2304]{0:T(1024)S(1)} fusion(f32[256]{0:T(256)S(1)} %bitcast.285, f32[256]{0:T(256)S(1)} %bitcast.277, f32[2304]{0:T(1024)S(1)} %get-tuple-element.382, f32[256]{0:T(256)S(1)} %bitcast.279, f32[256]{0:T(256)S(1)} %bitcast.281, f32[2304]{0:T(1024)S(1)} %get-tuple-element.385, f32[256]{0:T(256)S(1)} %bitcast.283, f32[256]{0:T(256)S(1)} %bitcast.275), kind=kLoop, calls=%fused_computation.26.clone.1.clone | loop fusion | flops 8255232 | bytes 33792 | tf_op jit(solution)/shard_map/while/body/eval_jaxpr/reduce_sum | solution.py:48
  50.8 4.6 %fusion.187 = f32[256,2304]{0,1:T(8,128)S(1)} fusion(f32[256]{0:T(256)S(1)} %bitcast.284, f32[256]{0:T(256)S(1)} %bitcast.276, f32[2304]{0:T(1024)S(1)} %get-tuple-element.382, f32[256]{0:T(256)S(1)} %bitcast.278, f32[256]{0:T(256)S(1)} %bitcast.280, f32[2304]{0:T(1024)S(1)} %get-tuple-element.385, f32[256]{0:T(256)S(1)} %bitcast.282, ...), kind=kOutput, calls=%fused_computation.19.clone.1.clone | convolution fusion | flops 1827405824 | bytes 2383872 | tf_op jit(solution)/shard_map/while/body/eval_jaxpr/dot_general | solution.py:45
  57.4 2.3 %fusion.186 = f32[2304]{0:T(1024)S(1)} fusion(f32[256]{0:T(256)S(1)} %bitcast.285, f32[256]{0:T(256)S(1)} %bitcast.277, f32[2304]{0:T(1024)S(1)} %get-tuple-element.382, f32[256]{0:T(256)S(1)} %bitcast.279, f32[256]{0:T(256)S(1)} %bitcast.281, f32[2304]{0:T(1024)S(1)} %get-tuple-element.385, f32[256]{0:T(256)S(1)} %bitcast.283, f32[256]{0:T(256)S(1)} %bitcast.275), kind=kLoop, calls=%fused_computation.26.clone.1.clone | loop fusion | flops 8255232 | bytes 33792 | tf_op jit(solution)/shard_map/while/body/eval_jaxpr/reduce_sum | solution.py:48
  60.4 57.0 %while.27 = (s32[]{:T(128)}, f32[3,9,256]{2,0,1:T(4,128)S(1)}, f32[3,9,256]{2,1,0:T(8,128)S(1)}, f32[3,4,2304]{2,1,0:T(4,128)S(1)}, f32[]{:T(128)}, /*index=5*/f32[]{:T(128)}) while((s32[]{:T(128)}, f32[3,9,256]{2,0,1:T(4,128)S(1)}, f32[3,9,256]{2,1,0:T(8,128)S(1)}, f32[3,4,2304]{2,1,0:T(4,128)S(1)}, ...), condition=%wide.region_6.7_spmd.clone.clone.clone, body=%wide.region_5.6_spmd.clone.clone.sunk.clone | while | flops 3743404544 | bytes 35934480 | solution.py:177
  61.8 4.9 %fusion.201 = f32[256,2304]{0,1:T(8,128)} fusion(f32[256]{0:T(256)S(1)} %bitcast.265, f32[256]{0:T(256)S(1)} %bitcast.256, f32[2304]{0:T(1024)S(1)} %get-tuple-element.410, f32[256]{0:T(256)S(1)} %bitcast.271, f32[256]{0:T(256)S(1)} %bitcast.259, f32[2304]{0:T(1024)S(1)} %get-tuple-element.409, f32[256]{0:T(256)S(1)} %bitcast.268, ...), kind=kOutput, calls=%fused_computation.66.clone.1.clone | convolution fusion | flops 1819738112 | bytes 2383872 | tf_op jit(solution)/shard_map/while/body/eval_jaxpr/dot_general | solution.py:102
  66.8 2.1 %fusion.200 = f32[256,2304]{0,1:T(8,128)S(1)} fusion(f32[3,4,2304]{2,1,0:T(4,128)S(1)} %get-tuple-element.469, s32[]{:T(128)} %get-tuple-element.460, f32[3,9,256]{2,1,0:T(8,128)S(1)} %get-tuple-element.468, s32[]{:T(128)S(6)} %add.601), kind=kOutput, calls=%fused_computation.88.clone.1.clone | convolution fusion | flops 21233664 | bytes 2401284 | tf_op jit(solution)/shard_map/while/body/eval_jaxpr/dot_general | solution.py:106
  68.9 4.4 %fusion.202 = f32[256,2304]{0,1:T(8,128)S(1)} fusion(f32[256,2304]{0,1:T(8,128)S(1)} %fusion.200, f32[256,2304]{0,1:T(8,128)S(1)} %copy-done.1, f32[2304]{0:T(1024)S(1)} %dynamic-slice_reduce_fusion.3, f32[256]{0:T(256)S(1)} %bitcast.266, f32[256]{0:T(256)S(1)} %bitcast.257, f32[2304]{0:T(1024)S(1)} %get-tuple-element.410, ...), kind=kOutput, calls=%fused_computation.70.clone.1.clone | convolution fusion | flops 1830944768 | bytes 7111680 | tf_op jit(solution)/shard_map/while/body/eval_jaxpr/dot_general | solution.py:113
  77.0 2.2 %fusion.205 = f32[3,256]{1,0:T(4,128)S(1)} fusion(f32[256,2304]{0,1:T(8,128)S(1)} %copy-done.2, f32[256]{0:T(256)S(1)} %bitcast.267, f32[256]{0:T(256)S(1)} %bitcast.258, f32[2304]{0:T(1024)S(1)} %get-tuple-element.410, f32[256]{0:T(256)S(1)} %bitcast.273, f32[256]{0:T(256)S(1)} %bitcast.261, f32[2304]{0:T(1024)S(1)} %get-tuple-element.409, ...), kind=kOutput, calls=%fused_computation.80.clone.1.clone | convolution fusion | flops 28901376 | bytes 2429956 | tf_op jit(solution)/shard_map/while/body/eval_jaxpr/dot_general | solution.py:63
  80.7 4.9 %fusion.201 = f32[256,2304]{0,1:T(8,128)} fusion(f32[256]{0:T(256)S(1)} %bitcast.265, f32[256]{0:T(256)S(1)} %bitcast.256, f32[2304]{0:T(1024)S(1)} %get-tuple-element.410, f32[256]{0:T(256)S(1)} %bitcast.271, f32[256]{0:T(256)S(1)} %bitcast.259, f32[2304]{0:T(1024)S(1)} %get-tuple-element.409, f32[256]{0:T(256)S(1)} %bitcast.268, ...), kind=kOutput, calls=%fused_computation.66.clone.1.clone | convolution fusion | flops 1819738112 | bytes 2383872 | tf_op jit(solution)/shard_map/while/body/eval_jaxpr/dot_general | solution.py:102
  87.8 4.4 %fusion.202 = f32[256,2304]{0,1:T(8,128)S(1)} fusion(f32[256,2304]{0,1:T(8,128)S(1)} %fusion.200, f32[256,2304]{0,1:T(8,128)S(1)} %copy-done.1, f32[2304]{0:T(1024)S(1)} %dynamic-slice_reduce_fusion.3, f32[256]{0:T(256)S(1)} %bitcast.266, f32[256]{0:T(256)S(1)} %bitcast.257, f32[2304]{0:T(1024)S(1)} %get-tuple-element.410, ...), kind=kOutput, calls=%fused_computation.70.clone.1.clone | convolution fusion | flops 1830944768 | bytes 7111680 | tf_op jit(solution)/shard_map/while/body/eval_jaxpr/dot_general | solution.py:113
  95.9 2.2 %fusion.205 = f32[3,256]{1,0:T(4,128)S(1)} fusion(f32[256,2304]{0,1:T(8,128)S(1)} %copy-done.2, f32[256]{0:T(256)S(1)} %bitcast.267, f32[256]{0:T(256)S(1)} %bitcast.258, f32[2304]{0:T(1024)S(1)} %get-tuple-element.410, f32[256]{0:T(256)S(1)} %bitcast.273, f32[256]{0:T(256)S(1)} %bitcast.261, f32[2304]{0:T(1024)S(1)} %get-tuple-element.409, ...), kind=kOutput, calls=%fused_computation.80.clone.1.clone | convolution fusion | flops 28901376 | bytes 2429956 | tf_op jit(solution)/shard_map/while/body/eval_jaxpr/dot_general | solution.py:63
  99.6 4.9 %fusion.201 = f32[256,2304]{0,1:T(8,128)} fusion(f32[256]{0:T(256)S(1)} %bitcast.265, f32[256]{0:T(256)S(1)} %bitcast.256, f32[2304]{0:T(1024)S(1)} %get-tuple-element.410, f32[256]{0:T(256)S(1)} %bitcast.271, f32[256]{0:T(256)S(1)} %bitcast.259, f32[2304]{0:T(1024)S(1)} %get-tuple-element.409, f32[256]{0:T(256)S(1)} %bitcast.268, ...), kind=kOutput, calls=%fused_computation.66.clone.1.clone | convolution fusion | flops 1819738112 | bytes 2383872 | tf_op jit(solution)/shard_map/while/body/eval_jaxpr/dot_general | solution.py:102
  104.5 2.1 %fusion.200 = f32[256,2304]{0,1:T(8,128)S(1)} fusion(f32[3,4,2304]{2,1,0:T(4,128)S(1)} %get-tuple-element.469, s32[]{:T(128)} %get-tuple-element.460, f32[3,9,256]{2,1,0:T(8,128)S(1)} %get-tuple-element.468, s32[]{:T(128)S(6)} %add.601), kind=kOutput, calls=%fused_computation.88.clone.1.clone | convolution fusion | flops 21233664 | bytes 2401284 | tf_op jit(solution)/shard_map/while/body/eval_jaxpr/dot_general | solution.py:106
  106.7 4.4 %fusion.202 = f32[256,2304]{0,1:T(8,128)S(1)} fusion(f32[256,2304]{0,1:T(8,128)S(1)} %fusion.200, f32[256,2304]{0,1:T(8,128)S(1)} %copy-done.1, f32[2304]{0:T(1024)S(1)} %dynamic-slice_reduce_fusion.3, f32[256]{0:T(256)S(1)} %bitcast.266, f32[256]{0:T(256)S(1)} %bitcast.257, f32[2304]{0:T(1024)S(1)} %get-tuple-element.410, ...), kind=kOutput, calls=%fused_computation.70.clone.1.clone | convolution fusion | flops 1830944768 | bytes 7111680 | tf_op jit(solution)/shard_map/while/body/eval_jaxpr/dot_general | solution.py:113
  114.7 2.2 %fusion.205 = f32[3,256]{1,0:T(4,128)S(1)} fusion(f32[256,2304]{0,1:T(8,128)S(1)} %copy-done.2, f32[256]{0:T(256)S(1)} %bitcast.267, f32[256]{0:T(256)S(1)} %bitcast.258, f32[2304]{0:T(1024)S(1)} %get-tuple-element.410, f32[256]{0:T(256)S(1)} %bitcast.273, f32[256]{0:T(256)S(1)} %bitcast.261, f32[2304]{0:T(1024)S(1)} %get-tuple-element.409, ...), kind=kOutput, calls=%fused_computation.80.clone.1.clone | convolution fusion | flops 28901376 | bytes 2429956 | tf_op jit(solution)/shard_map/while/body/eval_jaxpr/dot_general | solution.py:63
  120.6 2.6 %collective-permute-done.4 = f32[16,9,256]{2,0,1:T(8,128)S(1)} collective-permute-done((f32[16,9,256]{2,0,1:T(8,128)S(1)}, f32[16,9,256]{2,0,1:T(8,128)S(1)}, u32[]{:S(2)}, u32[]{:S(2)}) %collective-permute-start.4) | collective-permute-done | bytes 147488 | tf_op jit(solution)/shard_map/ppermute | solution.py:14
  124.1 2.9 %collective-permute-done.6 = f32[16,9,256]{2,0,1:T(8,128)S(1)} collective-permute-done((f32[16,9,256]{2,0,1:T(8,128)S(1)}, f32[16,9,256]{2,0,1:T(8,128)S(1)}, u32[]{:S(2)}, u32[]{:S(2)}) %collective-permute-start.6) | collective-permute-done | bytes 147488 | tf_op jit(solution)/shard_map/ppermute | solution.py:14
  127.0 2.2 %collective-permute-done.7 = f32[16,9,256]{2,0,1:T(8,128)S(1)} collective-permute-done((f32[16,9,256]{2,0,1:T(8,128)S(1)}, f32[16,9,256]{2,0,1:T(8,128)S(1)}, u32[]{:S(2)}, u32[]{:S(2)}) %collective-permute-start.7) | collective-permute-done | bytes 147488 | tf_op jit(solution)/shard_map/ppermute | solution.py:14
  130.5 44.9 %all-reduce.2.cloned.1.call-done = f32[16,9,256]{2,0,1:T(8,128)} async-done(((f32[16,9,256]{2,0,1:T(8,128)}), f32[16,9,256]{2,0,1:T(8,128)}) %all-reduce.2.cloned.1.call-update) | async-done | bytes 147472 | tf_op jit(solution)/shard_map/psum | solution.py:186
  (121 shorter events, 51.4 us)
Async XLA Ops:
  7.2 168.3 %all-reduce.2.cloned.1.call-start = ((), (), s32[]{:S(2)}) async-start(), calls=%async_computation | async-start | bytes 294912 | tf_op jit(solution)/shard_map/psum | solution.py:186
  8.2 13.0 %collective-permute-start = (f32[16,9,256]{2,1,0:T(8,128)S(1)}, f32[16,9,256]{2,1,0:T(8,128)S(1)}, u32[]{:S(2)}, u32[]{:S(2)}) collective-permute-start(f32[16,9,256]{2,1,0:T(8,128)S(1)} %copy.22), channel_id=1, source_target_pairs={{248,0},{252,4},{0,8},{4,12},{8,16},{12,20},{16,24},{20,28},{24,32... | collective-permute-start | bytes 442376 | tf_op jit(solution)/shard_map/ppermute | solution.py:14
  10.2 12.9 %collective-permute-start.1 = (f32[16,9,256]{2,1,0:T(8,128)S(1)}, f32[16,9,256]{2,1,0:T(8,128)S(1)}, u32[]{:S(2)}, u32[]{:S(2)}) collective-permute-start(f32[16,9,256]{2,1,0:T(8,128)S(1)} %copy.22), channel_id=1, source_target_pairs={{252,0},{0,4},{4,8},{8,12},{12,16},{16,20},{20,24},{24,28},{28,32}... | collective-permute-start | bytes 442376 | tf_op jit(solution)/shard_map/ppermute | solution.py:14
  10.2 15.4 %collective-permute-start.2 = (f32[16,9,256]{2,1,0:T(8,128)S(1)}, f32[16,9,256]{2,1,0:T(8,128)S(1)}, u32[]{:S(2)}, u32[]{:S(2)}) collective-permute-start(f32[16,9,256]{2,1,0:T(8,128)S(1)} %copy.22), channel_id=1, source_target_pairs={{4,0},{8,4},{12,8},{16,12},{20,16},{24,20},{28,24},{32,28},{36,32}... | collective-permute-start | bytes 442376 | tf_op jit(solution)/shard_map/ppermute | solution.py:14
  14.1 12.2 %collective-permute-start.3 = (f32[16,9,256]{2,1,0:T(8,128)S(1)}, f32[16,9,256]{2,1,0:T(8,128)S(1)}, u32[]{:S(2)}, u32[]{:S(2)}) collective-permute-start(f32[16,9,256]{2,1,0:T(8,128)S(1)} %copy.22), channel_id=1, source_target_pairs={{8,0},{12,4},{16,8},{20,12},{24,16},{28,20},{32,24},{36,28},{40,32... | collective-permute-start | bytes 442376 | tf_op jit(solution)/shard_map/ppermute | solution.py:14
  29.0 31.1 %copy-start = (f32[1,1,3,2304]{3,1,2,0:T(1,128)S(1)}, f32[1,1,3,2304]{3,1,2,0:T(1,128)}, u32[]{:S(2)}) copy-start(f32[1,1,3,2304]{3,1,2,0:T(1,128)} %param.15) | copy-start | bytes 82948
  66.8 2.2 %copy-start.1 = (f32[256,2304]{0,1:T(8,128)S(1)}, f32[256,2304]{0,1:T(8,128)}, u32[]{:S(2)}) copy-start(f32[256,2304]{0,1:T(8,128)} %fusion.201) | copy-start | bytes 7077892 | tf_op jit(solution)/shard_map/while
  75.3 1.7 copy-start.2
  85.6 2.2 %copy-start.1 = (f32[256,2304]{0,1:T(8,128)S(1)}, f32[256,2304]{0,1:T(8,128)}, u32[]{:S(2)}) copy-start(f32[256,2304]{0,1:T(8,128)} %fusion.201) | copy-start | bytes 7077892 | tf_op jit(solution)/shard_map/while
  94.2 1.7 copy-start.2
  104.5 2.2 %copy-start.1 = (f32[256,2304]{0,1:T(8,128)S(1)}, f32[256,2304]{0,1:T(8,128)}, u32[]{:S(2)}) copy-start(f32[256,2304]{0,1:T(8,128)} %fusion.201) | copy-start | bytes 7077892 | tf_op jit(solution)/shard_map/while
  113.1 1.7 copy-start.2
  118.0 5.2 %collective-permute-start.4 = (f32[16,9,256]{2,0,1:T(8,128)S(1)}, f32[16,9,256]{2,0,1:T(8,128)S(1)}, u32[]{:S(2)}, u32[]{:S(2)}) collective-permute-start(f32[16,9,256]{2,0,1:T(8,128)S(1)} %get-tuple-element.244), channel_id=1, source_target_pairs={{8,0},{12,4},{16,8},{20,12},{24,16},{28,20},{32,24},{36,28},{40,32... | collective-permute-start | bytes 442376 | tf_op jit(solution)/shard_map/ppermute | solution.py:14
  119.8 4.2 %collective-permute-start.5 = (f32[16,9,256]{2,0,1:T(8,128)S(1)}, f32[16,9,256]{2,0,1:T(8,128)S(1)}, u32[]{:S(2)}, u32[]{:S(2)}) collective-permute-start(f32[16,9,256]{2,0,1:T(8,128)S(1)} %get-tuple-element.247), channel_id=1, source_target_pairs={{4,0},{8,4},{12,8},{16,12},{20,16},{24,20},{28,24},{32,28},{36,32}... | collective-permute-start | bytes 442376 | tf_op jit(solution)/shard_map/ppermute | solution.py:14
  119.8 7.2 %collective-permute-start.6 = (f32[16,9,256]{2,0,1:T(8,128)S(1)}, f32[16,9,256]{2,0,1:T(8,128)S(1)}, u32[]{:S(2)}, u32[]{:S(2)}) collective-permute-start(f32[16,9,256]{2,0,1:T(8,128)S(1)} %get-tuple-element.246), channel_id=1, source_target_pairs={{252,0},{0,4},{4,8},{8,12},{12,16},{16,20},{20,24},{24,28},{28,32}... | collective-permute-start | bytes 442376 | tf_op jit(solution)/shard_map/ppermute | solution.py:14
  120.3 8.8 %collective-permute-start.7 = (f32[16,9,256]{2,0,1:T(8,128)S(1)}, f32[16,9,256]{2,0,1:T(8,128)S(1)}, u32[]{:S(2)}, u32[]{:S(2)}) collective-permute-start(f32[16,9,256]{2,0,1:T(8,128)S(1)} %get-tuple-element.245), channel_id=1, source_target_pairs={{248,0},{252,4},{0,8},{4,12},{8,16},{12,20},{16,24},{20,28},{24,32... | collective-permute-start | bytes 442376 | tf_op jit(solution)/shard_map/ppermute | solution.py:14
Sparse Core Ops, SparseCore 0:
  130.0 45.3 all-reduce.1
where the time goes:
time: 184 us
  matrix products  64.5 us (35%)
  waiting for transfers between devices  55.8 us (30%)
  other arithmetic  23.4 us (13%)
  between operations  15.5 us (8%)
  local copies, waits for them, and re-layouts  13.4 us (7%)
  starting transfers between devices  10.3 us (6%)
    psum x1, waiting for transfers between devices, shards(): gauss_grad = lax.psum(block_grads, 'view')  44.9 us
    dot_general x3, matrix products, backward_task(): jnp.dot(lower_tri, log_trans, precision=precise, preferred_element_type=j...  14.8 us
    dot_general x3, matrix products, forward_task(): jnp.dot(lower_tri, log_trans, precision=precise, preferred_element_type=j...  13.9 us
    dot_general x3, matrix products, backward_task(): jnp.dot(upper_tri, weights * shaded, precision=precise, preferred_element...  13.2 us
    ppermute x8, waiting for transfers between devices, shifted(): return lax.ppermute(block, axis, route)  10.9 us
    ppermute x8, starting transfers between devices, shifted(): return lax.ppermute(block, axis, route)  10.3 us
    sub x6, other arithmetic, pixel_frame(): pix_y = (pixel_ids // TILE).astype(jnp.float32) - centre - shift[1]  7.23 us
    reduce_sum x3, other arithmetic, forward_task(): totals = jnp.sum(log_trans, axis=0)  6.89 us
  transfers between devices with their start and end apart: 9, of which 7 were waited for; matrix products, arithmetic and copies ran while one was open for 4% of the time, Pallas kernels for 0%

commit v1 on v0

--- a/solution.py
+++ b/solution.py
@@ -183,7 +183,10 @@
     for shift_by in range(-REACH, REACH + 1):
         if shift_by != 0:
             block_grads = block_grads + shifted(spread[shift_by + REACH], "cell", shift_by)
-    gauss_grad = lax.psum(block_grads, "view")
+    devices_2, gauss_grad = (lax.axis_size("view"), block_grads)
+    for far in [1 << k for k in range(devices_2.bit_length() - 1)]:
+        pairs = [(i_2, i_2 ^ far) for i_2 in range(devices_2)]
+        gauss_grad = gauss_grad + lax.ppermute(gauss_grad, "view", pairs)
     return (rendered[None, None], gauss_grad)
 
 

time: 184 us -> 143 us (0.78)
  the two profiles are of different devices: /device:TPU:8 before, /device:TPU:6 now
where the time goes in v1:
time: 143 us
  matrix products  64.5 us (45%)
  other arithmetic  25.3 us (18%)
  waiting for transfers between devices  22.3 us (16%)
  starting transfers between devices  15.9 us (11%)
  local copies, waits for them, and re-layouts  11.8 us (8%)
  between operations  2.09 us (1%)
    dot_general x3, matrix products, backward_task(): jnp.dot(lower_tri, log_trans, precision=precise, preferred_element_type=j...  14.8 us
    dot_general x3, matrix products, forward_task(): jnp.dot(lower_tri, log_trans, precision=precise, preferred_element_type=j...  13.9 us
    ppermute x8, starting transfers between devices, shifted(): return lax.ppermute(block, axis, route)  13.5 us
    dot_general x3, matrix products, backward_task(): jnp.dot(upper_tri, weights * shaded, precision=precise, preferred_element...  13.2 us
    ppermute x8, waiting for transfers between devices, shifted(): return lax.ppermute(block, axis, route)  12.4 us
    ppermute x2, waiting for transfers between devices, shards(): gauss_grad = gauss_grad + lax.ppermute(gauss_grad, 'view', pairs)  9.93 us
    sub x6, other arithmetic, pixel_frame(): pix_y = (pixel_ids // TILE).astype(jnp.float32) - centre - shift[1]  8.23 us
    reduce_sum x3, other arithmetic, forward_task(): totals = jnp.sum(log_trans, axis=0)  6.88 us
  transfers between devices with their start and end apart: 10, of which 8 were waited for; matrix products, arithmetic and copies ran while one was open for 5% of the time, Pallas kernels for 0%

profile of v1, /device:TPU:6, one launch (start us, length us, event | category | flops | bytes accessed | tf_op | source)
XLA Modules:
  0.0 142.9 jit_solution(14372255164604053403)
XLA Ops:
  3.6 6.0 %collective-permute-start.2 = (f32[16,9,256]{2,1,0:T(8,128)S(1)}, f32[16,9,256]{2,1,0:T(8,128)S(1)}, u32[]{:S(2)}, u32[]{:S(2)}) collective-permute-start(f32[16,9,256]{2,1,0:T(8,128)S(1)} %copy.22), channel_id=1, source_target_pairs={{4,0},{8,4},{12,8},{16,12},{20,16},{24,20},{28,24},{32,28},{36,32}... | collective-permute-start | bytes 442376 | tf_op jit(solution)/shard_map/ppermute | solution.py:14
  9.6 2.2 %collective-permute-start.3 = (f32[16,9,256]{2,1,0:T(8,128)S(1)}, f32[16,9,256]{2,1,0:T(8,128)S(1)}, u32[]{:S(2)}, u32[]{:S(2)}) collective-permute-start(f32[16,9,256]{2,1,0:T(8,128)S(1)} %copy.22), channel_id=1, source_target_pairs={{8,0},{12,4},{16,8},{20,12},{24,16},{28,20},{32,24},{36,28},{40,32... | collective-permute-start | bytes 442376 | tf_op jit(solution)/shard_map/ppermute | solution.py:14
  24.9 31.3 %while.26 = (s32[]{:T(128)}, f32[3,4,2304]{2,1,0:T(4,128)S(1)}, f32[3,9,256]{2,1,0:T(8,128)S(1)}, f32[]{:T(128)}, f32[]{:T(128)}) while((s32[]{:T(128)}, f32[3,4,2304]{2,1,0:T(4,128)S(1)}, f32[3,9,256]{2,1,0:T(8,128)S(1)}, f32[]{:T(128)}, f32[]{:T(128)}) %tuple.102), condition=%wide.region_2.3_spmd.clone.clone, body=%wide.region_0.2_spmd.clone.sunk.clone | while | flops 1856945664 | bytes 4940977 | solution.py:173
  26.4 4.6 %fusion.187 = f32[256,2304]{0,1:T(8,128)S(1)} fusion(f32[256]{0:T(256)S(1)} %bitcast.284, f32[256]{0:T(256)S(1)} %bitcast.276, f32[2304]{0:T(1024)S(1)} %get-tuple-element.382, f32[256]{0:T(256)S(1)} %bitcast.278, f32[256]{0:T(256)S(1)} %bitcast.280, f32[2304]{0:T(1024)S(1)} %get-tuple-element.385, f32[256]{0:T(256)S(1)} %bitcast.282, ...), kind=kOutput, calls=%fused_computation.19.clone.1.clone | convolution fusion | flops 1827405824 | bytes 2383872 | tf_op jit(solution)/shard_map/while/body/eval_jaxpr/dot_general | solution.py:45
  33.0 2.3 %fusion.186 = f32[2304]{0:T(1024)S(1)} fusion(f32[256]{0:T(256)S(1)} %bitcast.285, f32[256]{0:T(256)S(1)} %bitcast.277, f32[2304]{0:T(1024)S(1)} %get-tuple-element.382, f32[256]{0:T(256)S(1)} %bitcast.279, f32[256]{0:T(256)S(1)} %bitcast.281, f32[2304]{0:T(1024)S(1)} %get-tuple-element.385, f32[256]{0:T(256)S(1)} %bitcast.283, f32[256]{0:T(256)S(1)} %bitcast.275), kind=kLoop, calls=%fused_computation.26.clone.1.clone | loop fusion | flops 8255232 | bytes 33792 | tf_op jit(solution)/shard_map/while/body/eval_jaxpr/reduce_sum | solution.py:48
  36.8 4.6 %fusion.187 = f32[256,2304]{0,1:T(8,128)S(1)} fusion(f32[256]{0:T(256)S(1)} %bitcast.284, f32[256]{0:T(256)S(1)} %bitcast.276, f32[2304]{0:T(1024)S(1)} %get-tuple-element.382, f32[256]{0:T(256)S(1)} %bitcast.278, f32[256]{0:T(256)S(1)} %bitcast.280, f32[2304]{0:T(1024)S(1)} %get-tuple-element.385, f32[256]{0:T(256)S(1)} %bitcast.282, ...), kind=kOutput, calls=%fused_computation.19.clone.1.clone | convolution fusion | flops 1827405824 | bytes 2383872 | tf_op jit(solution)/shard_map/while/body/eval_jaxpr/dot_general | solution.py:45
  43.4 2.3 %fusion.186 = f32[2304]{0:T(1024)S(1)} fusion(f32[256]{0:T(256)S(1)} %bitcast.285, f32[256]{0:T(256)S(1)} %bitcast.277, f32[2304]{0:T(1024)S(1)} %get-tuple-element.382, f32[256]{0:T(256)S(1)} %bitcast.279, f32[256]{0:T(256)S(1)} %bitcast.281, f32[2304]{0:T(1024)S(1)} %get-tuple-element.385, f32[256]{0:T(256)S(1)} %bitcast.283, f32[256]{0:T(256)S(1)} %bitcast.275), kind=kLoop, calls=%fused_computation.26.clone.1.clone | loop fusion | flops 8255232 | bytes 33792 | tf_op jit(solution)/shard_map/while/body/eval_jaxpr/reduce_sum | solution.py:48
  47.2 4.6 %fusion.187 = f32[256,2304]{0,1:T(8,128)S(1)} fusion(f32[256]{0:T(256)S(1)} %bitcast.284, f32[256]{0:T(256)S(1)} %bitcast.276, f32[2304]{0:T(1024)S(1)} %get-tuple-element.382, f32[256]{0:T(256)S(1)} %bitcast.278, f32[256]{0:T(256)S(1)} %bitcast.280, f32[2304]{0:T(1024)S(1)} %get-tuple-element.385, f32[256]{0:T(256)S(1)} %bitcast.282, ...), kind=kOutput, calls=%fused_computation.19.clone.1.clone | convolution fusion | flops 1827405824 | bytes 2383872 | tf_op jit(solution)/shard_map/while/body/eval_jaxpr/dot_general | solution.py:45
  53.9 2.3 %fusion.186 = f32[2304]{0:T(1024)S(1)} fusion(f32[256]{0:T(256)S(1)} %bitcast.285, f32[256]{0:T(256)S(1)} %bitcast.277, f32[2304]{0:T(1024)S(1)} %get-tuple-element.382, f32[256]{0:T(256)S(1)} %bitcast.279, f32[256]{0:T(256)S(1)} %bitcast.281, f32[2304]{0:T(1024)S(1)} %get-tuple-element.385, f32[256]{0:T(256)S(1)} %bitcast.283, f32[256]{0:T(256)S(1)} %bitcast.275), kind=kLoop, calls=%fused_computation.26.clone.1.clone | loop fusion | flops 8255232 | bytes 33792 | tf_op jit(solution)/shard_map/while/body/eval_jaxpr/reduce_sum | solution.py:48
  56.9 58.3 %while.27 = (s32[]{:T(128)}, f32[3,9,256]{2,0,1:T(4,128)S(1)}, f32[3,9,256]{2,1,0:T(8,128)S(1)}, f32[3,4,2304]{2,1,0:T(4,128)S(1)}, f32[]{:T(128)}, /*index=5*/f32[]{:T(128)}) while((s32[]{:T(128)}, f32[3,9,256]{2,0,1:T(4,128)S(1)}, f32[3,9,256]{2,1,0:T(8,128)S(1)}, f32[3,4,2304]{2,1,0:T(4,128)S(1)}, ...), condition=%wide.region_6.7_spmd.clone.clone.clone, body=%wide.region_5.6_spmd.clone.clone.sunk.clone | while | flops 3743404544 | bytes 35934480 | solution.py:177
  58.5 4.9 %fusion.201 = f32[256,2304]{0,1:T(8,128)} fusion(f32[256]{0:T(256)S(1)} %bitcast.265, f32[256]{0:T(256)S(1)} %bitcast.256, f32[2304]{0:T(1024)S(1)} %get-tuple-element.410, f32[256]{0:T(256)S(1)} %bitcast.271, f32[256]{0:T(256)S(1)} %bitcast.259, f32[2304]{0:T(1024)S(1)} %get-tuple-element.409, f32[256]{0:T(256)S(1)} %bitcast.268, ...), kind=kOutput, calls=%fused_computation.66.clone.1.clone | convolution fusion | flops 1819738112 | bytes 2383872 | tf_op jit(solution)/shard_map/while/body/eval_jaxpr/dot_general | solution.py:102
  65.6 4.4 %fusion.202 = f32[256,2304]{0,1:T(8,128)S(1)} fusion(f32[256,2304]{0,1:T(8,128)S(1)} %fusion.200, f32[256,2304]{0,1:T(8,128)S(1)} %copy-done.1, f32[2304]{0:T(1024)S(1)} %dynamic-slice_reduce_fusion.3, f32[256]{0:T(256)S(1)} %bitcast.266, f32[256]{0:T(256)S(1)} %bitcast.257, f32[2304]{0:T(1024)S(1)} %get-tuple-element.410, ...), kind=kOutput, calls=%fused_computation.70.clone.1.clone | convolution fusion | flops 1830944768 | bytes 7111680 | tf_op jit(solution)/shard_map/while/body/eval_jaxpr/dot_general | solution.py:113
  73.9 2.2 %fusion.205 = f32[3,256]{1,0:T(4,128)S(1)} fusion(f32[256,2304]{0,1:T(8,128)S(1)} %copy-done.2, f32[256]{0:T(256)S(1)} %bitcast.267, f32[256]{0:T(256)S(1)} %bitcast.258, f32[2304]{0:T(1024)S(1)} %get-tuple-element.410, f32[256]{0:T(256)S(1)} %bitcast.273, f32[256]{0:T(256)S(1)} %bitcast.261, f32[2304]{0:T(1024)S(1)} %get-tuple-element.409, ...), kind=kOutput, calls=%fused_computation.80.clone.1.clone | convolution fusion | flops 28901376 | bytes 2429956 | tf_op jit(solution)/shard_map/while/body/eval_jaxpr/dot_general | solution.py:63
  77.8 4.9 %fusion.201 = f32[256,2304]{0,1:T(8,128)} fusion(f32[256]{0:T(256)S(1)} %bitcast.265, f32[256]{0:T(256)S(1)} %bitcast.256, f32[2304]{0:T(1024)S(1)} %get-tuple-element.410, f32[256]{0:T(256)S(1)} %bitcast.271, f32[256]{0:T(256)S(1)} %bitcast.259, f32[2304]{0:T(1024)S(1)} %get-tuple-element.409, f32[256]{0:T(256)S(1)} %bitcast.268, ...), kind=kOutput, calls=%fused_computation.66.clone.1.clone | convolution fusion | flops 1819738112 | bytes 2383872 | tf_op jit(solution)/shard_map/while/body/eval_jaxpr/dot_general | solution.py:102
  84.9 4.4 %fusion.202 = f32[256,2304]{0,1:T(8,128)S(1)} fusion(f32[256,2304]{0,1:T(8,128)S(1)} %fusion.200, f32[256,2304]{0,1:T(8,128)S(1)} %copy-done.1, f32[2304]{0:T(1024)S(1)} %dynamic-slice_reduce_fusion.3, f32[256]{0:T(256)S(1)} %bitcast.266, f32[256]{0:T(256)S(1)} %bitcast.257, f32[2304]{0:T(1024)S(1)} %get-tuple-element.410, ...), kind=kOutput, calls=%fused_computation.70.clone.1.clone | convolution fusion | flops 1830944768 | bytes 7111680 | tf_op jit(solution)/shard_map/while/body/eval_jaxpr/dot_general | solution.py:113
  93.2 2.2 %fusion.205 = f32[3,256]{1,0:T(4,128)S(1)} fusion(f32[256,2304]{0,1:T(8,128)S(1)} %copy-done.2, f32[256]{0:T(256)S(1)} %bitcast.267, f32[256]{0:T(256)S(1)} %bitcast.258, f32[2304]{0:T(1024)S(1)} %get-tuple-element.410, f32[256]{0:T(256)S(1)} %bitcast.273, f32[256]{0:T(256)S(1)} %bitcast.261, f32[2304]{0:T(1024)S(1)} %get-tuple-element.409, ...), kind=kOutput, calls=%fused_computation.80.clone.1.clone | convolution fusion | flops 28901376 | bytes 2429956 | tf_op jit(solution)/shard_map/while/body/eval_jaxpr/dot_general | solution.py:63
  97.1 4.9 %fusion.201 = f32[256,2304]{0,1:T(8,128)} fusion(f32[256]{0:T(256)S(1)} %bitcast.265, f32[256]{0:T(256)S(1)} %bitcast.256, f32[2304]{0:T(1024)S(1)} %get-tuple-element.410, f32[256]{0:T(256)S(1)} %bitcast.271, f32[256]{0:T(256)S(1)} %bitcast.259, f32[2304]{0:T(1024)S(1)} %get-tuple-element.409, f32[256]{0:T(256)S(1)} %bitcast.268, ...), kind=kOutput, calls=%fused_computation.66.clone.1.clone | convolution fusion | flops 1819738112 | bytes 2383872 | tf_op jit(solution)/shard_map/while/body/eval_jaxpr/dot_general | solution.py:102
  104.2 4.4 %fusion.202 = f32[256,2304]{0,1:T(8,128)S(1)} fusion(f32[256,2304]{0,1:T(8,128)S(1)} %fusion.200, f32[256,2304]{0,1:T(8,128)S(1)} %copy-done.1, f32[2304]{0:T(1024)S(1)} %dynamic-slice_reduce_fusion.3, f32[256]{0:T(256)S(1)} %bitcast.266, f32[256]{0:T(256)S(1)} %bitcast.257, f32[2304]{0:T(1024)S(1)} %get-tuple-element.410, ...), kind=kOutput, calls=%fused_computation.70.clone.1.clone | convolution fusion | flops 1830944768 | bytes 7111680 | tf_op jit(solution)/shard_map/while/body/eval_jaxpr/dot_general | solution.py:113
  112.5 2.2 %fusion.205 = f32[3,256]{1,0:T(4,128)S(1)} fusion(f32[256,2304]{0,1:T(8,128)S(1)} %copy-done.2, f32[256]{0:T(256)S(1)} %bitcast.267, f32[256]{0:T(256)S(1)} %bitcast.258, f32[2304]{0:T(1024)S(1)} %get-tuple-element.410, f32[256]{0:T(256)S(1)} %bitcast.273, f32[256]{0:T(256)S(1)} %bitcast.261, f32[2304]{0:T(1024)S(1)} %get-tuple-element.409, ...), kind=kOutput, calls=%fused_computation.80.clone.1.clone | convolution fusion | flops 28901376 | bytes 2429956 | tf_op jit(solution)/shard_map/while/body/eval_jaxpr/dot_general | solution.py:63
  115.8 2.7 %collective-permute-start.4 = (f32[16,9,256]{2,0,1:T(8,128)S(1)}, f32[16,9,256]{2,0,1:T(8,128)S(1)}, u32[]{:S(2)}, u32[]{:S(2)}) collective-permute-start(f32[16,9,256]{2,0,1:T(8,128)S(1)} %get-tuple-element.244), channel_id=1, source_target_pairs={{8,0},{12,4},{16,8},{20,12},{24,16},{28,20},{32,24},{36,28},{40,32... | collective-permute-start | bytes 442376 | tf_op jit(solution)/shard_map/ppermute | solution.py:14
  122.8 4.1 %collective-permute-done.6 = f32[16,9,256]{2,0,1:T(8,128)S(1)} collective-permute-done((f32[16,9,256]{2,0,1:T(8,128)S(1)}, f32[16,9,256]{2,0,1:T(8,128)S(1)}, u32[]{:S(2)}, u32[]{:S(2)}) %collective-permute-start.6) | collective-permute-done | bytes 147488 | tf_op jit(solution)/shard_map/ppermute | solution.py:14
  127.0 2.2 %collective-permute-done.7 = f32[16,9,256]{2,0,1:T(8,128)S(1)} collective-permute-done((f32[16,9,256]{2,0,1:T(8,128)S(1)}, f32[16,9,256]{2,0,1:T(8,128)S(1)}, u32[]{:S(2)}, u32[]{:S(2)}) %collective-permute-start.7) | collective-permute-done | bytes 147488 | tf_op jit(solution)/shard_map/ppermute | solution.py:14
  130.1 5.2 %collective-permute-done.8 = f32[16,9,256]{2,0,1:T(8,128)S(1)} collective-permute-done((f32[16,9,256]{2,0,1:T(8,128)S(1)}, f32[16,9,256]{2,0,1:T(8,128)S(1)}, u32[]{:S(2)}, u32[]{:S(2)}) %collective-permute-start.8) | collective-permute-done | bytes 147488 | tf_op jit(solution)/shard_map/ppermute | solution.py:189
  137.5 4.7 %collective-permute-done.9 = f32[16,9,256]{2,0,1:T(8,128)S(1)} collective-permute-done((f32[16,9,256]{2,0,1:T(8,128)S(1)}, f32[16,9,256]{2,0,1:T(8,128)S(1)}, u32[]{:S(2)}, u32[]{:S(2)}) %collective-permute-start.9) | collective-permute-done | bytes 147488 | tf_op jit(solution)/shard_map/ppermute | solution.py:189
  (123 shorter events, 57.2 us)
Async XLA Ops:
  1.6 15.5 %collective-permute-start = (f32[16,9,256]{2,1,0:T(8,128)S(1)}, f32[16,9,256]{2,1,0:T(8,128)S(1)}, u32[]{:S(2)}, u32[]{:S(2)}) collective-permute-start(f32[16,9,256]{2,1,0:T(8,128)S(1)} %copy.22), channel_id=1, source_target_pairs={{248,0},{252,4},{0,8},{4,12},{8,16},{12,20},{16,24},{20,28},{24,32... | collective-permute-start | bytes 442376 | tf_op jit(solution)/shard_map/ppermute | solution.py:14
  3.6 15.5 %collective-permute-start.1 = (f32[16,9,256]{2,1,0:T(8,128)S(1)}, f32[16,9,256]{2,1,0:T(8,128)S(1)}, u32[]{:S(2)}, u32[]{:S(2)}) collective-permute-start(f32[16,9,256]{2,1,0:T(8,128)S(1)} %copy.22), channel_id=1, source_target_pairs={{252,0},{0,4},{4,8},{8,12},{12,16},{16,20},{20,24},{24,28},{28,32}... | collective-permute-start | bytes 442376 | tf_op jit(solution)/shard_map/ppermute | solution.py:14
  3.6 17.9 %collective-permute-start.2 = (f32[16,9,256]{2,1,0:T(8,128)S(1)}, f32[16,9,256]{2,1,0:T(8,128)S(1)}, u32[]{:S(2)}, u32[]{:S(2)}) collective-permute-start(f32[16,9,256]{2,1,0:T(8,128)S(1)} %copy.22), channel_id=1, source_target_pairs={{4,0},{8,4},{12,8},{16,12},{20,16},{24,20},{28,24},{32,28},{36,32}... | collective-permute-start | bytes 442376 | tf_op jit(solution)/shard_map/ppermute | solution.py:14
  9.6 12.6 %collective-permute-start.3 = (f32[16,9,256]{2,1,0:T(8,128)S(1)}, f32[16,9,256]{2,1,0:T(8,128)S(1)}, u32[]{:S(2)}, u32[]{:S(2)}) collective-permute-start(f32[16,9,256]{2,1,0:T(8,128)S(1)} %copy.22), channel_id=1, source_target_pairs={{8,0},{12,4},{16,8},{20,12},{24,16},{28,20},{32,24},{36,28},{40,32... | collective-permute-start | bytes 442376 | tf_op jit(solution)/shard_map/ppermute | solution.py:14
  24.9 31.6 %copy-start = (f32[1,1,3,2304]{3,1,2,0:T(1,128)S(1)}, f32[1,1,3,2304]{3,1,2,0:T(1,128)}, u32[]{:S(2)}) copy-start(f32[1,1,3,2304]{3,1,2,0:T(1,128)} %param.15) | copy-start | bytes 82948
  63.4 2.2 %copy-start.1 = (f32[256,2304]{0,1:T(8,128)S(1)}, f32[256,2304]{0,1:T(8,128)}, u32[]{:S(2)}) copy-start(f32[256,2304]{0,1:T(8,128)} %fusion.201) | copy-start | bytes 7077892 | tf_op jit(solution)/shard_map/while
  72.3 1.7 %copy-start.2 = (f32[256,2304]{0,1:T(8,128)S(1)}, f32[256,2304]{0,1:T(8,128)}, u32[]{:S(2)}) copy-start(f32[256,2304]{0,1:T(8,128)} %fusion.201) | copy-start | bytes 7077892 | tf_op jit(solution)/shard_map/while
  82.7 2.2 %copy-start.1 = (f32[256,2304]{0,1:T(8,128)S(1)}, f32[256,2304]{0,1:T(8,128)}, u32[]{:S(2)}) copy-start(f32[256,2304]{0,1:T(8,128)} %fusion.201) | copy-start | bytes 7077892 | tf_op jit(solution)/shard_map/while
  91.6 1.7 %copy-start.2 = (f32[256,2304]{0,1:T(8,128)S(1)}, f32[256,2304]{0,1:T(8,128)}, u32[]{:S(2)}) copy-start(f32[256,2304]{0,1:T(8,128)} %fusion.201) | copy-start | bytes 7077892 | tf_op jit(solution)/shard_map/while
  102.0 2.2 %copy-start.1 = (f32[256,2304]{0,1:T(8,128)S(1)}, f32[256,2304]{0,1:T(8,128)}, u32[]{:S(2)}) copy-start(f32[256,2304]{0,1:T(8,128)} %fusion.201) | copy-start | bytes 7077892 | tf_op jit(solution)/shard_map/while
  110.9 1.7 %copy-start.2 = (f32[256,2304]{0,1:T(8,128)S(1)}, f32[256,2304]{0,1:T(8,128)}, u32[]{:S(2)}) copy-start(f32[256,2304]{0,1:T(8,128)} %fusion.201) | copy-start | bytes 7077892 | tf_op jit(solution)/shard_map/while
  115.8 5.4 %collective-permute-start.4 = (f32[16,9,256]{2,0,1:T(8,128)S(1)}, f32[16,9,256]{2,0,1:T(8,128)S(1)}, u32[]{:S(2)}, u32[]{:S(2)}) collective-permute-start(f32[16,9,256]{2,0,1:T(8,128)S(1)} %get-tuple-element.244), channel_id=1, source_target_pairs={{8,0},{12,4},{16,8},{20,12},{24,16},{28,20},{32,24},{36,28},{40,32... | collective-permute-start | bytes 442376 | tf_op jit(solution)/shard_map/ppermute | solution.py:14
  118.6 4.2 %collective-permute-start.5 = (f32[16,9,256]{2,0,1:T(8,128)S(1)}, f32[16,9,256]{2,0,1:T(8,128)S(1)}, u32[]{:S(2)}, u32[]{:S(2)}) collective-permute-start(f32[16,9,256]{2,0,1:T(8,128)S(1)} %get-tuple-element.247), channel_id=1, source_target_pairs={{4,0},{8,4},{12,8},{16,12},{20,16},{24,20},{28,24},{32,28},{36,32}... | collective-permute-start | bytes 442376 | tf_op jit(solution)/shard_map/ppermute | solution.py:14
  118.6 8.4 %collective-permute-start.6 = (f32[16,9,256]{2,0,1:T(8,128)S(1)}, f32[16,9,256]{2,0,1:T(8,128)S(1)}, u32[]{:S(2)}, u32[]{:S(2)}) collective-permute-start(f32[16,9,256]{2,0,1:T(8,128)S(1)} %get-tuple-element.246), channel_id=1, source_target_pairs={{252,0},{0,4},{4,8},{8,12},{12,16},{16,20},{20,24},{24,28},{28,32}... | collective-permute-start | bytes 442376 | tf_op jit(solution)/shard_map/ppermute | solution.py:14
  119.1 10.0 %collective-permute-start.7 = (f32[16,9,256]{2,0,1:T(8,128)S(1)}, f32[16,9,256]{2,0,1:T(8,128)S(1)}, u32[]{:S(2)}, u32[]{:S(2)}) collective-permute-start(f32[16,9,256]{2,0,1:T(8,128)S(1)} %get-tuple-element.245), channel_id=1, source_target_pairs={{248,0},{252,4},{0,8},{4,12},{8,16},{12,20},{16,24},{20,28},{24,32... | collective-permute-start | bytes 442376 | tf_op jit(solution)/shard_map/ppermute | solution.py:14
  129.2 6.2 %collective-permute-start.8 = (f32[16,9,256]{2,0,1:T(8,128)S(1)}, f32[16,9,256]{2,0,1:T(8,128)S(1)}, u32[]{:S(2)}, u32[]{:S(2)}) collective-permute-start(f32[16,9,256]{2,0,1:T(8,128)S(1)} %fusion.110), channel_id=1, source_target_pairs={{0,1},{1,0},{2,3},{3,2},{4,5},{5,4},{6,7},{7,6},{8,9},{9,8},{10,11... | collective-permute-start | bytes 442376 | tf_op jit(solution)/shard_map/ppermute | solution.py:189
  135.4 6.8 %collective-permute-start.9 = (f32[16,9,256]{2,0,1:T(8,128)S(1)}, f32[16,9,256]{2,0,1:T(8,128)S(1)}, u32[]{:S(2)}, u32[]{:S(2)}) collective-permute-start(f32[16,9,256]{2,0,1:T(8,128)S(1)} %add.274), channel_id=1, source_target_pairs={{0,2},{1,3},{2,0},{3,1},{4,6},{5,7},{6,4},{7,5},{8,10},{9,11},{10,... | collective-permute-start | bytes 442376 | tf_op jit(solution)/shard_map/ppermute | solution.py:189
